TPU v7x, 512 devices: a whole 4x4x16 slice. The times are simulated.
512 devices in a mesh: rows: 64 (over x, z), cols: 8 (over y, core).
Axes of the slice: x: 4, y: 4, z: 16, core: 2. Of those that a mesh axis runs over, the one named last changes fastest.
Arguments:
- sketch: bfloat16 [131072, 256], P(('rows', 'cols')), may hold values from -6 to 6
- blocks: bfloat16 [4096, 256, 256], P(('rows', 'cols')), may hold values from -0.375 to 0.375
- block_rows: int32 [4096], P(('rows', 'cols')), may hold values from 0 to 3, as said below
- block_cols: int32 [4096], P(('rows', 'cols')), may hold values from 0 to 63
- counts: int32 [512], P(('rows', 'cols')), may hold values from 1 to 8, as said below
Outputs:
- basis: float32 [65536, 256], P(('rows', 'cols'))
- factor: float32 [256, 256], replicated
Inputs may be any that keep to these rules, and one draw needn't show every extreme that they name: Within one device's 8 slots the pairs (block_rows, block_cols) are distinct. `counts`: some device has exactly 8 live slots.
All inputs are finite; a program needn't handle non-finite values.
Results may differ from a plain program's by a relative error of at most 0.0003.
Values may be sent and summed in bfloat16 or wider, within the bound.
A program may use at most 64 MiB of HBM per device.

v0:
```python
import jax
import jax.numpy as jnp
from jax import lax
from jax.sharding import PartitionSpec as P

RB = 4


def local(sketch, blocks, block_rows, block_cols, counts):
    highest = lax.Precision.HIGHEST
    slots, width, _ = blocks.shape
    columns = sketch.shape[1]
    live_count = counts[0]
    starts = block_cols * width
    panel = lax.all_gather(sketch, "rows", axis=0, tiled=True)
    chosen = jax.vmap(lambda offset: lax.dynamic_slice_in_dim(panel, offset, width, 0))(starts)
    products = jnp.einsum("bij,bjk->bik", blocks, chosen, preferred_element_type=jnp.float32)
    selector = (
        (block_rows[:, None] == jnp.arange(RB, dtype=jnp.int32)[None, :])
        & (jnp.arange(slots, dtype=jnp.int32) < live_count)[:, None]
    ).astype(jnp.float32)
    partial_rows = jnp.einsum("br,bik->rik", selector, products, precision=highest)
    partial_rows = partial_rows.reshape(RB * width, columns)
    total_rows = RB * width * lax.axis_size("rows")
    slab_total = lax.psum(partial_rows, "cols")
    gram_matrix = lax.psum(jnp.dot(slab_total.T, slab_total, precision=highest), "rows")
    share_rows = slab_total.shape[0] // lax.axis_size("cols")
    own_rows = lax.dynamic_slice_in_dim(
        slab_total, lax.axis_index("cols") * share_rows, share_rows, 0
    )
    lower_factor = jnp.linalg.cholesky(gram_matrix)
    root_rows = jnp.sqrt(jnp.float32(total_rows))
    solved = lax.linalg.triangular_solve(
        lower_factor, own_rows, left_side=False, lower=True, transpose_a=True
    )
    return (solved * root_rows, lower_factor.T / root_rows)


def solution(mesh):
    in_specs = (
        P(("rows", "cols"), None),
        P(("rows", "cols"), None, None),
        P(("rows", "cols")),
        P(("rows", "cols")),
        P(("rows", "cols")),
    )
    out_specs = (P(("rows", "cols"), None), P())
    return jax.shard_map(local, mesh=mesh, in_specs=in_specs, out_specs=out_specs, check_vma=False)
```

profile of v0, /device:TPU:8, one launch (start us, length us, event | category | flops | bytes accessed | tf_op | source)
XLA Modules:
  0.0 611.1 jit_solution(694707326038857665)
XLA Ops:
  7.2 0.7 all-gather.2.cloned.1.call-update
  9.3 162.0 %all-gather.2.cloned.1.call-done = bf16[16384,256]{1,0:T(8,128)(2,1)} async-done(((bf16[256,256]{1,0:T(8,128)(2,1)}), bf16[16384,256]{1,0:T(8,128)(2,1)}) %all-gather.2.cloned.1.call-update) | async-done | bytes 8388624 | tf_op jit(solution)/shard_map/all_gather | solution.py:15
  171.3 17.0 %while.2 = (s32[]{:T(128)}, bf16[16384,256]{1,0:T(8,128)(2,1)}, s32[8,2]{0,1:T(2,128)S(1)}, bf16[8,256,256]{2,1,0:T(8,128)(2,1)S(1)}, s32[]{:T(128)}) while((s32[]{:T(128)}, bf16[16384,256]{1,0:T(8,128)(2,1)}, s32[8,2]{0,1:T(2,128)S(1)}, bf16[8,256,256]{2,1,0:T(8,128)(2,1)S(1)}, s32[]{:T(128)}) %tuple.41), condition=%wide.while_cond, body=%wide.while_body.sunk | while | flops 2 | bytes 262241 | solution.py:16
  171.9 1.5 bitcast_dynamic-update-slice_fusion.4
  174.0 1.5 bitcast_dynamic-update-slice_fusion.4
  176.2 1.5 bitcast_dynamic-update-slice_fusion.4
  178.3 1.5 bitcast_dynamic-update-slice_fusion.4
  180.4 1.5 bitcast_dynamic-update-slice_fusion.4
  182.6 1.5 bitcast_dynamic-update-slice_fusion.4
  184.7 1.5 bitcast_dynamic-update-slice_fusion.4
  186.8 1.5 bitcast_dynamic-update-slice_fusion.4
  188.4 1.8 fusion.19
  190.2 2.2 copy.16
  192.4 1.1 fusion
  193.5 1.2 copy.11
  195.0 70.9 %all-reduce.5.cloned.1.call-done = f32[1024,256]{1,0:T(8,128)} async-done(((f32[1024,256]{1,0:T(8,128)}), f32[1024,256]{1,0:T(8,128)}) %all-reduce.5.cloned.1.call-update) | async-done | bytes 1048592 | tf_op jit(solution)/shard_map/psum | solution.py:25
  265.9 4.1 fusion.20
  270.0 268.6 %all-reduce.7.cloned.1.call-done = f32[256,256]{0,1:T(8,128)} async-done(((f32[256,256]{0,1:T(8,128)}), f32[256,256]{0,1:T(8,128)}) %all-reduce.7.cloned.1.call-update) | async-done | bytes 262160 | tf_op jit(solution)/shard_map/psum | solution.py:26
  538.6 1.1 copy.13
  539.6 1.0 fusion.2
  540.6 11.7 %cholesky.50 = f32[128,128]{1,0:T(8,128)S(1)} custom-call(f32[128,128]{1,0:T(8,128)S(1)} %cholesky.118), custom_call_target="Cholesky" | custom-call | tf_op jit(solution)/shard_map/jit(cholesky)/cholesky | solution.py:31
  552.4 9.8 %custom-call.14 = f32[1,128,128]{1,2,0:T(8,128)S(1)} custom-call(f32[1,128,128]{2,1,0:T(8,128)S(1)} %get-tuple-element.45), custom_call_target="InvertDiagBlocksLowerTriangular" | custom-call | tf_op jit(solution)/shard_map/jit(cholesky)/cholesky | solution.py:31
  562.7 11.7 %cholesky.105 = f32[128,128]{1,0:T(8,128)S(1)} custom-call(f32[128,128]{1,0:T(8,128)S(1)} %convolution_subtract_fusion.1), custom_call_target="Cholesky" | custom-call | tf_op jit(solution)/shard_map/jit(cholesky)/cholesky | solution.py:31
  574.5 0.8 compare_reduce_fusion
  576.7 4.0 while.3
  577.3 1.4 bitcast_dynamic-update-slice_fusion.5
  579.3 1.4 bitcast_dynamic-update-slice_fusion.5
  580.7 19.7 %custom-call.15 = f32[2,128,128]{1,2,0:T(8,128)S(1)} custom-call(f32[2,128,128]{2,1,0:T(8,128)S(1)} %get-tuple-element.17), custom_call_target="InvertDiagBlocksLowerTriangular" | custom-call | tf_op jit(solution)/shard_map/triangular_solve | solution.py:33
  600.4 1.1 fusion.6
  601.5 1.1 convolution_subtract_fusion
  603.0 0.8 copy.14
  603.7 0.8 copy.15
  (45 shorter events, 7.9 us)
Async XLA Ops:
  7.2 181.2 %copy-start = (bf16[8,256,256]{2,1,0:T(8,128)(2,1)S(1)}, bf16[8,256,256]{2,1,0:T(8,128)(2,1)}, u32[]{:S(2)}) copy-start(bf16[8,256,256]{2,1,0:T(8,128)(2,1)} %param.6) | copy-start | bytes 3145732
  7.2 164.1 %all-gather.2.cloned.1.call-start = ((), (), s32[]{:S(2)}) async-start(), calls=%async_computation | async-start | bytes 8519680 | tf_op jit(solution)/shard_map/all_gather | solution.py:15
  7.9 258.0 %all-reduce.5.cloned.1.call-start = ((), (), s32[]{:S(2)}) async-start(), calls=%async_computation.1 | async-start | bytes 2097152 | tf_op jit(solution)/shard_map/psum | solution.py:25
  190.2 2.2 copy-start.1
  194.8 343.8 %all-reduce.7.cloned.1.call-start = ((), (), s32[]{:S(2)}) async-start(), calls=%async_computation.2 | async-start | bytes 524288 | tf_op jit(solution)/shard_map/psum | solution.py:26
Sparse Core Ops, SparseCore 0:
  10.9 160.3 all-gather.1
  194.9 70.9 all-reduce.4
  270.1 268.4 all-reduce.6
where the time goes:
time: 612 us; the launch traced here: 611 us
  waiting for transfers between devices  502 us (82%)
  other arithmetic  55.5 us (9%)
  local copies, waits for them, and re-layouts  27 us (4%)
  between operations  15.9 us (3%)
  matrix products  10 us (2%)
    psum x1, waiting for transfers between devices, local(): lax.psum(jnp.dot(slab_total.T, slab_total, precision=highest), 'rows')  269 us
    all_gather x1, waiting for transfers between devices, local(): panel = lax.all_gather(sketch, 'rows', axis=0, tiled=True)  162 us
    psum x1, waiting for transfers between devices, local(): slab_total = lax.psum(partial_rows, 'cols')  70.9 us
    another operation x6, other arithmetic, local(): lower_factor = jnp.linalg.cholesky(gram_matrix)  34.2 us
    another operation x2, other arithmetic, local(): lax.linalg.triangular_solve(lower_factor, own_rows, left_side=False, lowe...  19.7 us
    gather x24, local copies, waits for them, and re-layouts  16.9 us
  transfers between devices with their start and end apart: 3, of which 3 were waited for; matrix products, arithmetic and copies ran while one was open for 0% of the time, Pallas kernels for 0%

commit v1 on v0

--- a/solution.py
+++ b/solution.py
@@ -12,7 +12,13 @@
     columns = sketch.shape[1]
     live_count = counts[0]
     starts = block_cols * width
-    panel = lax.all_gather(sketch, "rows", axis=0, tiled=True)
+    _direct_panels = lambda content: jnp.concatenate(
+        lax.all_to_all(
+            jnp.stack([content for _ in range(lax.axis_size("rows"))], axis=0), "rows", 0, 0
+        ),
+        axis=0,
+    )
+    panel = _direct_panels(sketch)
     chosen = jax.vmap(lambda offset: lax.dynamic_slice_in_dim(panel, offset, width, 0))(starts)
     products = jnp.einsum("bij,bjk->bik", blocks, chosen, preferred_element_type=jnp.float32)
     selector = (

time: 612 us -> 838 us (1.37)
  waiting for transfers between devices: 502 us -> 705 us
  starting transfers between devices: 0.3 us -> 19.2 us
    all_to_all x0 -> x1, waiting for transfers between devices: none -> 367 us  [local(): lax.all_to_all(jnp.stack([content for _ in range(lax.axis_size('rows'))],...]
    all_gather x1 -> x0, waiting for transfers between devices: 162 us -> none  [local(): panel = lax.all_gather(sketch, 'rows', axis=0, tiled=True)]
    all_to_all x0 -> x1, starting transfers between devices: none -> 19 us  [local(): lax.all_to_all(jnp.stack([content for _ in range(lax.axis_size('rows'))],...]
where the time goes in v1:
time: 838 us; the launch traced here: 837 us
  waiting for transfers between devices  705 us (84%)
  other arithmetic  54.9 us (7%)
  local copies, waits for them, and re-layouts  32.3 us (4%)
  starting transfers between devices  19.2 us (2%)
  between operations  16.2 us (2%)
  matrix products  10 us (1%)
    all_to_all x1, waiting for transfers between devices, local(): lax.all_to_all(jnp.stack([content for _ in range(lax.axis_size('rows'))],...  367 us
    psum x1, waiting for transfers between devices, local(): lax.psum(jnp.dot(slab_total.T, slab_total, precision=highest), 'rows')  269 us
    psum x1, waiting for transfers between devices, local(): slab_total = lax.psum(partial_rows, 'cols')  69.2 us
    another operation x6, other arithmetic, local(): lower_factor = jnp.linalg.cholesky(gram_matrix)  34.2 us
    another operation x2, other arithmetic, local(): lax.linalg.triangular_solve(lower_factor, own_rows, left_side=False, lowe...  19.7 us
    all_to_all x1, starting transfers between devices, local(): lax.all_to_all(jnp.stack([content for _ in range(lax.axis_size('rows'))],...  19 us
    gather x24, local copies, waits for them, and re-layouts  16.9 us
  transfers between devices with their start and end apart: 3, of which 3 were waited for; matrix products, arithmetic and copies ran while one was open for 0% of the time, Pallas kernels for 0%

profile of v1, /device:TPU:8, one launch (start us, length us, event | category | flops | bytes accessed | tf_op | source)
XLA Modules:
  0.0 837.3 jit_solution(13469405474299308735)
XLA Ops:
  7.2 5.2 stack.2
  12.4 19.0 %all-to-all-start = ((bf16[64,256,256]{2,1,0:T(8,128)(2,1)}), bf16[64,256,256]{2,1,0:T(8,128)(2,1)}, u32[]{:S(2)}, u32[]{:S(2)}) async-start(bf16[64,256,256]{2,1,0:T(8,128)(2,1)} %stack.2), calls=%async_computation | async-start | bytes 16777216 | tf_op jit(solution)/shard_map/all_to_all | solution.py:16
  32.1 366.8 %all-to-all-done = bf16[64,256,256]{2,1,0:T(8,128)(2,1)} async-done(((bf16[64,256,256]{2,1,0:T(8,128)(2,1)}), bf16[64,256,256]{2,1,0:T(8,128)(2,1)}, u32[]{:S(2)}, u32[]{:S(2)}) %all-to-all-start) | async-done | bytes 8388640 | tf_op jit(solution)/shard_map/all_to_all | solution.py:16
  399.0 17.0 %while.2 = (s32[]{:T(128)}, bf16[16384,256]{1,0:T(8,128)(2,1)}, s32[8,2]{0,1:T(2,128)S(1)}, bf16[8,256,256]{2,1,0:T(8,128)(2,1)S(1)}, s32[]{:T(128)}) while((s32[]{:T(128)}, bf16[16384,256]{1,0:T(8,128)(2,1)}, s32[8,2]{0,1:T(2,128)S(1)}, bf16[8,256,256]{2,1,0:T(8,128)(2,1)S(1)}, s32[]{:T(128)}) %tuple.41), condition=%wide.while_cond, body=%wide.while_body.sunk | while | flops 2 | bytes 262241 | solution.py:22
  399.5 1.5 bitcast_dynamic-update-slice_fusion.4
  401.7 1.5 bitcast_dynamic-update-slice_fusion.4
  403.8 1.5 bitcast_dynamic-update-slice_fusion.4
  405.9 1.5 bitcast_dynamic-update-slice_fusion.4
  408.1 1.5 bitcast_dynamic-update-slice_fusion.4
  410.2 1.5 bitcast_dynamic-update-slice_fusion.4
  412.3 1.5 bitcast_dynamic-update-slice_fusion.4
  414.5 1.5 bitcast_dynamic-update-slice_fusion.4
  416.0 1.8 fusion.19
  417.8 2.2 copy.16
  420.1 1.1 fusion
  421.2 1.2 copy.11
  422.6 69.2 %all-reduce.5.cloned.1.call-done = f32[1024,256]{1,0:T(8,128)} async-done(((f32[1024,256]{1,0:T(8,128)}), f32[1024,256]{1,0:T(8,128)}) %all-reduce.5.cloned.1.call-update) | async-done | bytes 1048592 | tf_op jit(solution)/shard_map/psum | solution.py:31
  491.8 4.1 fusion.20
  495.9 268.6 %all-reduce.7.cloned.1.call-done = f32[256,256]{0,1:T(8,128)} async-done(((f32[256,256]{0,1:T(8,128)}), f32[256,256]{0,1:T(8,128)}) %all-reduce.7.cloned.1.call-update) | async-done | bytes 262160 | tf_op jit(solution)/shard_map/psum | solution.py:32
  764.5 1.1 copy.13
  765.6 1.0 fusion.2
  766.6 11.7 %cholesky.50 = f32[128,128]{1,0:T(8,128)S(1)} custom-call(f32[128,128]{1,0:T(8,128)S(1)} %cholesky.118), custom_call_target="Cholesky" | custom-call | tf_op jit(solution)/shard_map/jit(cholesky)/cholesky | solution.py:37
  778.3 9.8 %custom-call.14 = f32[1,128,128]{1,2,0:T(8,128)S(1)} custom-call(f32[1,128,128]{2,1,0:T(8,128)S(1)} %get-tuple-element.45), custom_call_target="InvertDiagBlocksLowerTriangular" | custom-call | tf_op jit(solution)/shard_map/jit(cholesky)/cholesky | solution.py:37
  788.6 11.7 %cholesky.105 = f32[128,128]{1,0:T(8,128)S(1)} custom-call(f32[128,128]{1,0:T(8,128)S(1)} %convolution_subtract_fusion.1), custom_call_target="Cholesky" | custom-call | tf_op jit(solution)/shard_map/jit(cholesky)/cholesky | solution.py:37
  800.4 0.8 compare_reduce_fusion
  802.6 4.0 while.3
  803.2 1.4 bitcast_dynamic-update-slice_fusion.5
  805.2 1.4 bitcast_dynamic-update-slice_fusion.5
  806.6 19.7 %custom-call.15 = f32[2,128,128]{1,2,0:T(8,128)S(1)} custom-call(f32[2,128,128]{2,1,0:T(8,128)S(1)} %get-tuple-element.17), custom_call_target="InvertDiagBlocksLowerTriangular" | custom-call | tf_op jit(solution)/shard_map/triangular_solve | solution.py:39
  826.3 1.1 fusion.6
  827.4 1.1 convolution_subtract_fusion
  829.6 0.8 copy.15
  (47 shorter events, 8.0 us)
Async XLA Ops:
  7.2 408.8 %copy-start = (bf16[8,256,256]{2,1,0:T(8,128)(2,1)S(1)}, bf16[8,256,256]{2,1,0:T(8,128)(2,1)}, u32[]{:S(2)}) copy-start(bf16[8,256,256]{2,1,0:T(8,128)(2,1)} %param.6) | copy-start | bytes 3145732
  12.4 19.0 %copy-start.2 = (s32[8]{0:T(128)S(1)}, s32[8]{0:T(128)}, u32[]{:S(2)}) copy-start(s32[8]{0:T(128)} %param.8) | copy-start | bytes 100
  12.4 386.6 %all-to-all-start = ((bf16[64,256,256]{2,1,0:T(8,128)(2,1)}), bf16[64,256,256]{2,1,0:T(8,128)(2,1)}, u32[]{:S(2)}, u32[]{:S(2)}) async-start(bf16[64,256,256]{2,1,0:T(8,128)(2,1)} %stack.2), calls=%async_computation | async-start | bytes 16777216 | tf_op jit(solution)/shard_map/all_to_all | solution.py:16
  31.4 460.4 %all-reduce.5.cloned.1.call-start = ((), (), s32[]{:S(2)}) async-start(), calls=%async_computation.1 | async-start | bytes 2097152 | tf_op jit(solution)/shard_map/psum | solution.py:31
  417.8 2.2 copy-start.1
  422.4 342.1 %all-reduce.7.cloned.1.call-start = ((), (), s32[]{:S(2)}) async-start(), calls=%async_computation.2 | async-start | bytes 524288 | tf_op jit(solution)/shard_map/psum | solution.py:32
Sparse Core Ops, SparseCore 0:
  422.5 69.2 all-reduce.4
  496.0 268.4 all-reduce.6

commit v2 on v0

--- a/solution.py
+++ b/solution.py
@@ -22,7 +22,8 @@
     partial_rows = jnp.einsum("br,bik->rik", selector, products, precision=highest)
     partial_rows = partial_rows.reshape(RB * width, columns)
     total_rows = RB * width * lax.axis_size("rows")
-    slab_total = lax.psum(partial_rows, "cols")
+    parts = lax.all_gather(partial_rows, "cols", axis=0, tiled=False)
+    slab_total = parts.sum(axis=0)
     gram_matrix = lax.psum(jnp.dot(slab_total.T, slab_total, precision=highest), "rows")
     share_rows = slab_total.shape[0] // lax.axis_size("cols")
     own_rows = lax.dynamic_slice_in_dim(

time: 612 us -> 592 us (0.967)
  waiting for transfers between devices: 502 us -> 482 us
    psum x1 -> x0, waiting for transfers between devices: 70.9 us -> none  [local(): slab_total = lax.psum(partial_rows, 'cols')]
    all_gather x0 -> x1, waiting for transfers between devices: none -> 51.5 us  [local(): parts = lax.all_gather(partial_rows, 'cols', axis=0, tiled=False)]
where the time goes in v2:
time: 592 us
  waiting for transfers between devices  482 us (81%)
  other arithmetic  59.6 us (10%)
  local copies, waits for them, and re-layouts  27.1 us (5%)
  between operations  15.9 us (3%)
  matrix products  6.78 us (1%)
    psum x1, waiting for transfers between devices, local(): lax.psum(jnp.dot(slab_total.T, slab_total, precision=highest), 'rows')  268 us
    all_gather x1, waiting for transfers between devices, local(): panel = lax.all_gather(sketch, 'rows', axis=0, tiled=True)  162 us
    all_gather x1, waiting for transfers between devices, local(): parts = lax.all_gather(partial_rows, 'cols', axis=0, tiled=False)  51.5 us
    another operation x6, other arithmetic, local(): lower_factor = jnp.linalg.cholesky(gram_matrix)  34.2 us
    another operation x2, other arithmetic, local(): lax.linalg.triangular_solve(lower_factor, own_rows, left_side=False, lowe...  19.7 us
    gather x24, local copies, waits for them, and re-layouts  16.9 us
  transfers between devices with their start and end apart: 3, of which 3 were waited for; matrix products, arithmetic and copies ran while one was open for 0% of the time, Pallas kernels for 0%

profile of v2, /device:TPU:8, one launch (start us, length us, event | category | flops | bytes accessed | tf_op | source)
XLA Modules:
  0.0 592.0 jit_solution(18172097485865483841)
XLA Ops:
  7.2 0.7 all-gather.3.cloned.1.call-update
  8.0 0.7 fusion.15
  9.3 162.0 %all-gather.3.cloned.1.call-done = bf16[16384,256]{1,0:T(8,128)(2,1)} async-done(((bf16[256,256]{1,0:T(8,128)(2,1)}), bf16[16384,256]{1,0:T(8,128)(2,1)}) %all-gather.3.cloned.1.call-update) | async-done | bytes 8388624 | tf_op jit(solution)/shard_map/all_gather | solution.py:15
  171.3 17.0 %while.2 = (s32[]{:T(128)}, bf16[16384,256]{1,0:T(8,128)(2,1)}, s32[8,2]{0,1:T(2,128)S(1)}, bf16[8,256,256]{2,1,0:T(8,128)(2,1)S(1)}, s32[]{:T(128)}) while((s32[]{:T(128)}, bf16[16384,256]{1,0:T(8,128)(2,1)}, s32[8,2]{0,1:T(2,128)S(1)}, bf16[8,256,256]{2,1,0:T(8,128)(2,1)S(1)}, s32[]{:T(128)}) %tuple.42), condition=%wide.while_cond, body=%wide.while_body.sunk | while | flops 2 | bytes 262241 | solution.py:16
  171.9 1.5 bitcast_dynamic-update-slice_fusion.4
  174.0 1.5 bitcast_dynamic-update-slice_fusion.4
  176.2 1.5 bitcast_dynamic-update-slice_fusion.4
  178.3 1.5 bitcast_dynamic-update-slice_fusion.4
  180.4 1.5 bitcast_dynamic-update-slice_fusion.4
  182.6 1.5 bitcast_dynamic-update-slice_fusion.4
  184.7 1.5 bitcast_dynamic-update-slice_fusion.4
  186.8 1.5 bitcast_dynamic-update-slice_fusion.4
  188.4 1.8 convolution_bitcast_fusion
  190.2 2.2 copy.17
  192.4 1.1 fusion.11
  193.5 1.2 copy.18
  195.0 51.5 %all-gather.5.cloned.1.call-done = f32[8,1024,256]{2,1,0:T(8,128)} async-done(((f32[1,1024,256]{2,1,0:T(8,128)}), f32[8,1024,256]{2,1,0:T(8,128)}) %all-gather.5.cloned.1.call-update) | async-done | bytes 8388624 | tf_op jit(solution)/shard_map/all_gather | solution.py:25
  246.5 4.1 reduce_sum.9
  250.6 2.5 fusion.18
  253.2 267.9 %all-reduce.4.cloned.1.call-done = f32[256,256]{0,1:T(8,128)} async-done(((f32[256,256]{0,1:T(8,128)}), f32[256,256]{0,1:T(8,128)}) %all-reduce.4.cloned.1.call-update) | async-done | bytes 262160 | tf_op jit(solution)/shard_map/psum | solution.py:27
  521.1 1.1 copy.20
  522.2 1.0 fusion
  523.2 11.7 %cholesky.50 = f32[128,128]{1,0:T(8,128)S(1)} custom-call(f32[128,128]{1,0:T(8,128)S(1)} %cholesky.118), custom_call_target="Cholesky" | custom-call | tf_op jit(solution)/shard_map/jit(cholesky)/cholesky | solution.py:32
  535.0 9.8 %custom-call.14 = f32[1,128,128]{1,2,0:T(8,128)S(1)} custom-call(f32[1,128,128]{2,1,0:T(8,128)S(1)} %get-tuple-element.47), custom_call_target="InvertDiagBlocksLowerTriangular" | custom-call | tf_op jit(solution)/shard_map/jit(cholesky)/cholesky | solution.py:32
  545.3 11.9 %cholesky.105 = f32[128,128]{1,0:T(8,128)S(1)} custom-call(f32[128,128]{1,0:T(8,128)S(1)} %convolution_subtract_fusion.1), custom_call_target="Cholesky" | custom-call | tf_op jit(solution)/shard_map/jit(cholesky)/cholesky | solution.py:32
  557.2 0.7 compare_reduce_fusion
  559.3 4.0 while.3
  559.9 1.4 bitcast_dynamic-update-slice_fusion.5
  561.9 1.4 bitcast_dynamic-update-slice_fusion.5
  563.3 19.7 %custom-call.15 = f32[2,128,128]{1,2,0:T(8,128)S(1)} custom-call(f32[2,128,128]{2,1,0:T(8,128)S(1)} %get-tuple-element.17), custom_call_target="InvertDiagBlocksLowerTriangular" | custom-call | tf_op jit(solution)/shard_map/triangular_solve | solution.py:34
  583.8 0.8 copy.21
  584.6 0.8 copy.22
  (46 shorter events, 7.9 us)
Async XLA Ops:
  7.2 181.2 %copy-start = (bf16[8,256,256]{2,1,0:T(8,128)(2,1)S(1)}, bf16[8,256,256]{2,1,0:T(8,128)(2,1)}, u32[]{:S(2)}) copy-start(bf16[8,256,256]{2,1,0:T(8,128)(2,1)} %param.6) | copy-start | bytes 3145732
  7.2 164.1 %all-gather.3.cloned.1.call-start = ((), (), s32[]{:S(2)}) async-start(), calls=%async_computation | async-start | bytes 8519680 | tf_op jit(solution)/shard_map/all_gather | solution.py:15
  7.9 238.6 %all-gather.5.cloned.1.call-start = ((), (), s32[]{:S(2)}) async-start(), calls=%async_computation.1 | async-start | bytes 9437184 | tf_op jit(solution)/shard_map/all_gather | solution.py:25
  190.2 2.2 copy-start.1
  194.8 326.3 %all-reduce.4.cloned.1.call-start = ((), (), s32[]{:S(2)}) async-start(), calls=%async_computation.2 | async-start | bytes 524288 | tf_op jit(solution)/shard_map/psum | solution.py:27
Sparse Core Ops, SparseCore 0:
  10.9 160.3 all-gather.2
  194.9 51.5 all-gather.4
  253.3 267.7 all-reduce.3
